TPU v7x, 32 devices: a whole 2x2x4 slice. The times are simulated.
32 devices in a mesh: seg: 2 (over x), rows: 16 (over z, y, core).
Axes of the slice: x: 2, y: 2, z: 4, core: 2. Of those that a mesh axis runs over, the one named last changes fastest.
Arguments:
- snapshots: float32 [512, 131072], P('seg', 'rows'), parts along dimension 0, may hold values from -400 to 400
Outputs:
- q_panel: float32 [64, 131072], P('seg', 'rows'), parts along dimension 0
- r_panel: float32 [64, 32], P('seg'), parts along dimension 0
- projected: float32 [64, 224], P('seg'), parts along dimension 0
- trailing: float32 [448, 131072], P('seg', 'rows'), parts along dimension 0
There are 2 independent parts, one for each index of `seg`. A program takes and returns all parts, laid end to end along the dimension named above; each array names one. Nothing has to cross between parts.
All inputs are finite; a program needn't handle non-finite values.
Results may differ from a plain program's by a relative error of at most 0.000082.
Values sent between devices are 32-bit elements; how exact they have to be, the bound alone decides.
A program may use at most 64 MiB of HBM per device.

v0:
```python
import jax
import jax.numpy as jnp
from jax import lax
from jax.sharding import PartitionSpec as P

PANEL = 32


def inner(left, right):
    return lax.dot_general(
        left,
        right,
        (((1,), (1,)), ((), ())),
        precision=lax.Precision.HIGHEST,
        preferred_element_type=jnp.float32,
    )


def local(snapshots):
    panel = snapshots[:PANEL]
    rest = snapshots[PANEL:]
    totals = lax.psum(inner(panel, snapshots), "rows")
    lower = jnp.linalg.cholesky(totals[:, :PANEL])
    q_panel = jax.scipy.linalg.solve_triangular(lower, panel, lower=True)
    projected = jax.scipy.linalg.solve_triangular(lower, totals[:, PANEL:], lower=True)
    update = lax.dot_general(
        projected,
        q_panel,
        (((0,), (0,)), ((), ())),
        precision=lax.Precision.HIGHEST,
        preferred_element_type=jnp.float32,
    )
    trailing = rest - update
    return (q_panel, lower.T, projected, trailing)


def solution(mesh):
    return jax.shard_map(
        local,
        mesh=mesh,
        in_specs=(P("seg", "rows"),),
        out_specs=(P("seg", "rows"), P("seg", None), P("seg", None), P("seg", "rows")),
        check_vma=False,
    )
```

profile of v0, /device:TPU:0, one launch (start us, length us, event | category | flops | bytes accessed | tf_op | source)
XLA Modules:
  0.0 94.1 jit_solution(7879214852546602777)
XLA Ops:
  0.6 9.2 %fusion.2 = f32[32,256]{0,1:T(8,128)S(1)} fusion(f32[256,8192]{1,0:T(8,128)} %param.1), kind=kOutput, calls=%fused_computation.3 | convolution fusion | flops 805306368 | bytes 9469952 | tf_op jit(solution)/shard_map/dot_general | solution.py:10
  9.8 63.8 %psum.7 = f32[32,256]{0,1:T(8,128)S(1)} all-reduce(f32[32,256]{0,1:T(8,128)S(1)} %fusion.2), channel_id=1, replica_groups=mesh['seg'=2,'rows'=16] {'rows'}, use_global_device_ids=true, to_apply=%region_0.0 | all-reduce | flops 8192 | bytes 65536 | tf_op jit(solution)/shard_map/psum | solution.py:22
  73.6 0.1 copy.6
  73.7 2.9 %cholesky.16 = f32[32,32]{1,0:T(8,128)S(1)} custom-call(f32[32,32]{1,0:T(8,128)S(1)} %fusion.8), custom_call_target="Cholesky" | custom-call | tf_op jit(solution)/shard_map/jit(cholesky)/cholesky | solution.py:23
  76.6 0.6 compare_reduce_fusion
  77.3 0.7 fusion.9
  78.0 0.7 copy.7
  78.6 2.4 %custom-call.10 = f32[1,32,32]{1,2,0:T(8,128)S(1)} custom-call(f32[1,32,32]{2,1,0:T(8,128)S(1)} %get-tuple-element.9), custom_call_target="InvertDiagBlocksLowerTriangular" | custom-call | tf_op jit(solution)/shard_map/jit(_solve_triangular)/triangular_solve | solution.py:24
  81.1 0.4 fusion.4
  81.4 0.0 copy-start.1
  81.4 2.3 %fusion = f32[32,8192]{1,0:T(8,128)S(1)} fusion(f32[256,8192]{1,0:T(8,128)} %param.1, f32[1,32,32]{1,2,0:T(8,128)S(1)} %custom-call.10), kind=kOutput, calls=%fused_computation.1 | convolution fusion | flops 100663296 | bytes 2101248 | tf_op jit(solution)/shard_map/jit(_solve_triangular)/triangular_solve | solution.py:24
  83.7 0.0 copy-start
  83.7 10.4 %convolution_subtract_fusion = f32[224,8192]{1,0:T(8,128)} fusion(f32[32,224]{1,0:T(8,128)S(1)} %fusion.4, f32[32,8192]{1,0:T(8,128)S(1)} %fusion, f32[256,8192]{1,0:T(8,128)} %param.1), kind=kOutput, calls=%fused_computation | convolution fusion | flops 706478080 | bytes 15757312 | tf_op jit(solution)/shard_map/dot_general | solution.py:26
  94.1 0.0 copy-done.1
  94.1 0.0 copy-done
  (3 shorter events, 0.0 us)
Async XLA Ops:
  81.4 12.7 %copy-start.1 = (f32[32,224]{1,0:T(8,128)}, f32[32,224]{1,0:T(8,128)S(1)}, u32[]{:S(2)}) copy-start(f32[32,224]{1,0:T(8,128)S(1)} %fusion.4) | copy-start | bytes 86020
  83.7 10.4 %copy-start = (f32[32,8192]{1,0:T(8,128)}, f32[32,8192]{1,0:T(8,128)S(1)}, u32[]{:S(2)}) copy-start(f32[32,8192]{1,0:T(8,128)S(1)} %fusion) | copy-start | bytes 3145732
where the time goes:
time: 94.3 us; the launch traced here: 94.1 us
  blocking collectives  63.8 us (68%)
  matrix products  22.2 us (24%)
  other arithmetic  6.69 us (7%)
    psum x1, blocking collectives, local(): totals = lax.psum(inner(panel, snapshots), 'rows')  63.8 us
    dot_general x1, matrix products, local(): lax.dot_general(projected, q_panel, (((0,), (0,)), ((), ())), precision=l...  10.4 us
    dot_general x1, matrix products, inner(): lax.dot_general(left, right, (((1,), (1,)), ((), ())), precision=lax.Prec...  9.17 us
    another operation x3, other arithmetic, local(): lower = jnp.linalg.cholesky(totals[:, :PANEL])  3.6 us
    another operation x1, other arithmetic, local(): q_panel = jax.scipy.linalg.solve_triangular(lower, panel, lower=True)  2.44 us
    another operation x1, matrix products, local(): q_panel = jax.scipy.linalg.solve_triangular(lower, panel, lower=True)  2.26 us

commit v1 on v0

--- a/solution.py
+++ b/solution.py
@@ -19,7 +19,7 @@
 def local(snapshots):
     panel = snapshots[:PANEL]
     rest = snapshots[PANEL:]
-    totals = lax.psum(inner(panel, snapshots), "rows")
+    totals = jnp.sum(lax.all_gather(inner(panel, snapshots), "rows"), axis=0)
     lower = jnp.linalg.cholesky(totals[:, :PANEL])
     q_panel = jax.scipy.linalg.solve_triangular(lower, panel, lower=True)
     projected = jax.scipy.linalg.solve_triangular(lower, totals[:, PANEL:], lower=True)

time: 94.3 us -> 57 us (0.60)
  blocking collectives: 63.8 us -> 24.6 us
  matrix products: 22.2 us -> 24 us
    psum x1 -> x0, blocking collectives: 63.8 us -> none  [local(): totals = lax.psum(inner(panel, snapshots), 'rows')]
    all_gather x0 -> x1, blocking collectives: none -> 24.6 us  [local(): totals = jnp.sum(lax.all_gather(inner(panel, snapshots), 'rows'), axis=0)]
    dot_general x1, matrix products: 9.17 us -> 11.1 us  [inner(): lax.dot_general(left, right, (((1,), (1,)), ((), ())), precision=lax.Prec...]
where the time goes in v1:
time: 57 us; the launch traced here: 56.8 us
  blocking collectives  24.6 us (43%)
  matrix products  24 us (42%)
  other arithmetic  6.72 us (12%)
  local copies, waits for them, and re-layouts  0.77 us (1%)
  between operations  0.69 us (1%)
    all_gather x1, blocking collectives, local(): totals = jnp.sum(lax.all_gather(inner(panel, snapshots), 'rows'), axis=0)  24.6 us
    dot_general x1, matrix products, inner(): lax.dot_general(left, right, (((1,), (1,)), ((), ())), precision=lax.Prec...  11.1 us
    dot_general x1, matrix products, local(): lax.dot_general(projected, q_panel, (((0,), (0,)), ((), ())), precision=l...  10.4 us
    another operation x3, other arithmetic, local(): lower = jnp.linalg.cholesky(totals[:, :PANEL])  3.6 us
    another operation x1, other arithmetic, local(): q_panel = jax.scipy.linalg.solve_triangular(lower, panel, lower=True)  2.44 us
    another operation x1, matrix products, local(): q_panel = jax.scipy.linalg.solve_triangular(lower, panel, lower=True)  2.26 us

profile of v1, /device:TPU:0, one launch (start us, length us, event | category | flops | bytes accessed | tf_op | source)
XLA Modules:
  0.0 56.8 jit_solution(11678917172209085594)
XLA Ops:
  0.6 11.1 %fusion.2 = f32[32,256]{1,0:T(8,128)S(1)} fusion(f32[256,8192]{1,0:T(8,128)} %param.1), kind=kOutput, calls=%fused_computation.3 | convolution fusion | flops 805306368 | bytes 9469952 | tf_op jit(solution)/shard_map/dot_general | solution.py:10
  11.7 24.6 %all-gather = f32[512,256]{1,0:T(8,128)S(1)} all-gather(f32[32,256]{1,0:T(8,128)S(1)} %fusion.2), channel_id=2, replica_groups=mesh['seg'=2,'rows'=16] {'rows'}, dimensions={0}, use_global_device_ids=true | all-gather | bytes 557056 | tf_op jit(solution)/shard_map/all_gather | solution.py:22
  36.4 0.1 copy.10
  36.4 2.9 %cholesky.16 = f32[32,32]{1,0:T(8,128)S(1)} custom-call(f32[32,32]{1,0:T(8,128)S(1)} %fusion.8), custom_call_target="Cholesky" | custom-call | tf_op jit(solution)/shard_map/jit(cholesky)/cholesky | solution.py:23
  39.4 0.6 %compare_reduce_fusion = pred[]{:T(512)} fusion(f32[32]{0:T(128)S(1)} %select_reduce_fusion), kind=kLoop, calls=%fused_computation.17 | loop fusion | flops 63 | bytes 129 | tf_op jit(solution)/shard_map/jit(cholesky)/cholesky | solution.py:23
  40.0 0.7 %fusion.9 = (f32[32,32]{0,1:T(8,128)S(1)}, f32[1,32,32]{2,1,0:T(8,128)S(1)}) fusion(f32[32,32]{1,0:T(8,128)S(1)} %cholesky.16, pred[]{:T(512)} %compare_reduce_fusion), kind=kLoop, calls=%fused_computation.16 | loop fusion | flops 4096 | bytes 12289 | tf_op jit(solution)/shard_map/transpose | solution.py:34
  40.7 0.7 %copy.9 = f32[32,32]{1,0:T(8,128)} copy(f32[32,32]{0,1:T(8,128)S(1)} %get-tuple-element.12) | data formatting | bytes 8192
  41.4 2.4 %custom-call.10 = f32[1,32,32]{1,2,0:T(8,128)S(1)} custom-call(f32[1,32,32]{2,1,0:T(8,128)S(1)} %get-tuple-element.13), custom_call_target="InvertDiagBlocksLowerTriangular" | custom-call | tf_op jit(solution)/shard_map/jit(_solve_triangular)/triangular_solve | solution.py:24
  43.8 0.3 fusion.4
  44.1 0.0 copy-start.1
  44.1 2.3 %fusion = f32[32,8192]{1,0:T(8,128)S(1)} fusion(f32[256,8192]{1,0:T(8,128)} %param.1, f32[1,32,32]{1,2,0:T(8,128)S(1)} %custom-call.10), kind=kOutput, calls=%fused_computation.1 | convolution fusion | flops 100663296 | bytes 2101248 | tf_op jit(solution)/shard_map/jit(_solve_triangular)/triangular_solve | solution.py:24
  46.4 0.0 copy-start
  46.4 10.4 %convolution_subtract_fusion = f32[224,8192]{1,0:T(8,128)} fusion(f32[32,224]{1,0:T(8,128)S(1)} %fusion.4, f32[32,8192]{1,0:T(8,128)S(1)} %fusion, f32[256,8192]{1,0:T(8,128)} %param.1), kind=kOutput, calls=%fused_computation | convolution fusion | flops 706478080 | bytes 15757312 | tf_op jit(solution)/shard_map/dot_general | solution.py:26
  56.8 0.0 copy-done.1
  56.8 0.0 copy-done
  (4 shorter events, 0.1 us)
Async XLA Ops:
  44.1 12.7 %copy-start.1 = (f32[32,224]{1,0:T(8,128)}, f32[32,224]{1,0:T(8,128)S(1)}, u32[]{:S(2)}) copy-start(f32[32,224]{1,0:T(8,128)S(1)} %fusion.4) | copy-start | bytes 86020
  46.4 10.4 %copy-start = (f32[32,8192]{1,0:T(8,128)}, f32[32,8192]{1,0:T(8,128)S(1)}, u32[]{:S(2)}) copy-start(f32[32,8192]{1,0:T(8,128)S(1)} %fusion) | copy-start | bytes 3145732
